TPU v7x, 128 devices: a whole 4x4x4 slice. The times are simulated.
128 devices in a mesh: stream: 16 (over z, y), passage: 4 (over x_hi, core), span: 2 (over x_lo).
Axes of the slice: x: 4 (x_hi: 2, x_lo: 2; x = x_hi * 2 + x_lo), y: 4, z: 4, core: 2. Of those that a mesh axis runs over, the one named last changes fastest.
Arguments:
- residual: float32 [6, 32, 256, 256], P(None, 'stream', 'passage', 'span'), may hold values from -4 to 4
- dq_old: float32 [6, 32, 256, 256], P(None, 'stream', 'passage', 'span'), may hold values from -6 to 6
- lateral_coef: float32 [32, 256, 256], P('stream', 'passage', 'span'), may hold values from 0.05 to 0.25
- diag_inverse: float32 [6, 6, 32, 256, 256], P(None, None, 'stream', 'passage', 'span'), may hold values from -1 to 1.2, as said below
- match_list: int32 [16, 256], P('stream', 'passage'), may hold values from 0 to 255, as said below
- slide_weight: float32 [256], P('passage'), may hold values from 0 to 1
Outputs:
- dq_new: float32 [6, 32, 256, 256], P(None, 'stream', 'passage', 'span')
Inputs may be any that keep to these rules, and one draw needn't show every extreme that they name: match_list[b, p] = (p + offset_b) mod 256, where offset_b = (offset_0 + b * 64) mod 256. `diag_inverse`: each 6x6 block is a diagonal scaling of the identity plus a small antisymmetric part.
All inputs are finite; a program needn't handle non-finite values.
Results may differ from a plain program's by a relative error of at most 0.00013.
Values sent between devices are 32-bit elements; how exact they have to be, the bound alone decides.
No kernel may reach another device: no remote copies, remote signals or barrier semaphores. Data moves between devices by JAX's collectives and lax.ppermute only.
A program may use at most 320 MiB of HBM per device.

v0:
```python
import jax
import jax.numpy as jnp
from jax import lax
from jax.sharding import PartitionSpec as P


def padded(x, sides, width, wrap):
    for axis, dim in sides:
        peers, length = (lax.axis_size(axis), x.shape[dim])
        up = [(i, (i + 1) % peers) for i in range(peers if wrap else peers - 1)]
        down = [(j, i) for i, j in up]
        last = lax.slice_in_dim(x, length - width, length, axis=dim)
        first = lax.slice_in_dim(x, 0, width, axis=dim)
        before = lax.ppermute(last, axis, up)
        after = lax.ppermute(first, axis, down)
        x = jnp.concatenate([before, x, after], axis=dim)
    return x


def passed_along(block, axis, distance):
    devices = range(lax.axis_size(axis))
    route = [((i - distance) % len(devices), i) for i in devices]
    return lax.ppermute(block, axis, route)


def shifted(block, axis, distance):
    devices = range(lax.axis_size(axis))
    route = [(i - distance, i) for i in devices if i - distance in devices]
    return lax.ppermute(block, axis, route)


def apply_block(matrix, vector):
    return jnp.einsum("ab...,b...->a...", matrix, vector, precision=lax.Precision.HIGHEST)


def compose(later, earlier):
    return jnp.einsum("ab...,bc...->ac...", later, earlier, precision=lax.Precision.HIGHEST)


def plane_of(array, index, target_axis):
    return lax.dynamic_index_in_dim(array, index, target_axis, False)


def on_device(residual, dq_old, lateral_coef, diag_inverse, match_list, slide_weight):
    planes = residual.shape[1]
    beside_all = padded(dq_old, (("passage", 2),), 1, True)
    beside = padded(dq_old, (("span", 3),), 1, False)
    neighbours = (
        beside_all[:, :, 2:] + beside_all[:, :, :-2] + beside[:, :, :, 2:] + beside[:, :, :, :-2]
    )
    source = residual - lateral_coef[None] * neighbours
    face = dq_old[:, planes - 1]
    annulus = lax.all_gather(face, "passage", axis=1, tiled=True)
    upstream = passed_along(annulus, "stream", 1)
    total = upstream.shape[1]
    donors = match_list[0]
    nextidx = (donors + 1) % total
    weight = slide_weight[None, :, None]
    term = (1.0 - weight) * jnp.take(upstream, donors, axis=1) + weight * jnp.take(
        upstream, nextidx, axis=1
    )
    source = source.at[:, 0].add(term)
    first_inverse = diag_inverse[:, :, 0]
    start_maps = (first_inverse, apply_block(first_inverse, source[:, 0]))

    def lower_compose(index, carry):
        inverse = plane_of(diag_inverse, index, 2)
        given = plane_of(source, index, 1)
        return (compose(inverse, carry[0]), apply_block(inverse, carry[1] + given))

    lower_maps = lax.fori_loop(1, planes, lower_compose, start_maps)
    blocks = lax.axis_size("stream")

    def lower_pass(index, incoming):
        leaving = apply_block(lower_maps[0], incoming) + lower_maps[1]
        return shifted(leaving, "stream", 1)

    lower_in = lax.fori_loop(0, blocks - 1, lower_pass, jnp.zeros_like(lower_maps[1]))

    def lower_sweep(index, carry):
        current, lowers = carry
        inverse = plane_of(diag_inverse, index, 2)
        current = apply_block(inverse, plane_of(source, index, 1) + current)
        return (current, lax.dynamic_update_index_in_dim(lowers, current, index, 1))

    _, lowers = lax.fori_loop(0, planes, lower_sweep, (lower_in, jnp.zeros_like(source)))
    last_inverse = diag_inverse[:, :, planes - 1]
    top_maps = (last_inverse, lowers[:, planes - 1])

    def upper_compose(step, carry):
        index = planes - 1 - step
        inverse = plane_of(diag_inverse, index, 2)
        return (
            compose(inverse, carry[0]),
            plane_of(lowers, index, 1) + apply_block(inverse, carry[1]),
        )

    upper_maps = lax.fori_loop(1, planes, upper_compose, top_maps)

    def upper_pass(index, incoming):
        leaving = apply_block(upper_maps[0], incoming) + upper_maps[1]
        return shifted(leaving, "stream", -1)

    upper_in = lax.fori_loop(0, blocks - 1, upper_pass, jnp.zeros_like(upper_maps[1]))

    def upper_sweep(step, carry):
        current, uppers = carry
        index = planes - 1 - step
        inverse = plane_of(diag_inverse, index, 2)
        current = plane_of(lowers, index, 1) + apply_block(inverse, current)
        return (current, lax.dynamic_update_index_in_dim(uppers, current, index, 1))

    _, uppers = lax.fori_loop(0, planes, upper_sweep, (upper_in, jnp.zeros_like(source)))
    return uppers


def solution(mesh):
    placed = (
        P(None, "stream", "passage", "span"),
        P(None, "stream", "passage", "span"),
        P("stream", "passage", "span"),
        P(None, None, "stream", "passage", "span"),
        P("stream", "passage"),
        P("passage"),
    )
    return jax.shard_map(
        on_device,
        mesh=mesh,
        in_specs=placed,
        out_specs=P(None, "stream", "passage", "span"),
        check_vma=False,
    )
```

profile of v0, /device:TPU:24, one launch (start us, length us, event | category | flops | bytes accessed | tf_op | source)
XLA Modules:
  0.0 680.0 jit_solution(18425378000636333673)
XLA Ops:
  3.8 5.4 collective-permute-start.5
  12.3 15.9 %all-gather = f32[6,1,256,128]{3,1,0,2:T(1,128)S(1)} all-gather(f32[6,1,64,128]{3,1,0,2:T(1,128)S(1)} %copy.144), channel_id=2, replica_groups=mesh['stream'=16,'passage'=4,'span'=2] {'passage'}, dimensions={2}, use_global_device_ids=true | all-gather | bytes 983040 | tf_op jit(solution)/shard_map/all_gather | solution.py:53
  32.2 14.8 %copy.143 = f32[6,6,1,64,128]{1,0,4,3,2:T(8,128)} copy(f32[6,6,1,64,128]{4,3,2,1,0:T(8,128)} %get-tuple-element.438) | data formatting | bytes 2359296
  47.0 14.9 %copy.142 = f32[6,6,1,64,128]{0,1,4,3,2:T(8,128)} copy(f32[6,6,1,64,128]{4,3,2,1,0:T(8,128)} %get-tuple-element.437) | data formatting | bytes 2359296
  62.0 71.8 %fusion.17 = f32[6,6,64,128]{0,1,3,2:T(8,128)} fusion(f32[6,6,1,64,128]{0,1,4,3,2:T(8,128)} %copy.142, f32[6,6,1,64,128]{1,0,4,3,2:T(8,128)} %copy.143), kind=kOutput, calls=%fused_computation.28 | convolution fusion | flops 21233664 | bytes 3538944 | tf_op jit(solution)/shard_map/while/body/eval_jaxpr/ab...,bc...->ac.../dot_general | solution.py:37
  133.8 61.7 %fusion.12 = f32[6,6,64,128]{0,1,3,2:T(8,128)} fusion(f32[6,6,1,64,128]{1,0,4,3,2:T(8,128)} %copy.143, f32[6,6,1,64,128]{0,1,4,3,2:T(8,128)} %copy.142), kind=kOutput, calls=%fused_computation.27 | convolution fusion | flops 21233664 | bytes 3538944 | tf_op jit(solution)/shard_map/while/body/eval_jaxpr/ab...,bc...->ac.../dot_general | solution.py:37
  195.7 15.6 %copy.82 = f32[6,6,64,128]{3,2,1,0:T(8,128)} copy(f32[6,6,64,128]{0,1,3,2:T(8,128)} %fusion.17) | data formatting | bytes 2359296 | tf_op jit(solution)/shard_map/while | solution.py:78
  211.3 15.4 %copy.85 = f32[6,6,64,128]{3,2,1,0:T(8,128)} copy(f32[6,6,64,128]{0,1,3,2:T(8,128)} %fusion.12) | data formatting | bytes 2359296 | tf_op jit(solution)/shard_map/while | solution.py:104
  240.3 15.3 %fusion.4 = f32[64,128,6]{2,1,0:T(8,128)} fusion(f32[6,6,1,64,128]{1,0,4,3,2:T(8,128)} %copy.143, f32[64,128,6]{2,1,0:T(8,128)} %copy.145), kind=kLoop, calls=%fused_computation.19 | loop fusion | flops 540672 | bytes 1572864
  263.2 16.8 %fusion.3 = f32[64,128,6]{2,1,0:T(8,128)} fusion(f32[6,6,1,64,128]{0,1,4,3,2:T(8,128)} %copy.142, f32[64,128,6]{2,1,0:T(8,128)} %copy.146), kind=kLoop, calls=%fused_computation.16 | loop fusion | flops 540672 | bytes 1572864
  282.9 170.6 %while.65 = (s32[]{:T(128)}, f32[6,64,128]{2,1,0:T(8,128)S(1)}, f32[6,6,64,128]{3,2,1,0:T(8,128)}, f32[6,64,128]{2,1,0:T(8,128)S(1)}, s32[]{:T(128)}) while((s32[]{:T(128)}, f32[6,64,128]{2,1,0:T(8,128)S(1)}, f32[6,6,64,128]{3,2,1,0:T(8,128)}, f32[6,64,128]{2,1,0:T(8,128)S(1)}, s32[]{:T(128)}) %tuple.133), condition=%wide.region_1.3_spmd, body=%wide.region_0.2_spmd.sunk | while | flops 589826 | bytes 2949221 | solution.py:78
  287.9 5.8 collective-permute-done
  295.1 5.6 collective-permute-start
  300.7 4.0 collective-permute-done
  306.1 6.5 collective-permute-start
  317.2 6.5 collective-permute-start
  328.4 6.5 collective-permute-start
  339.5 6.5 collective-permute-start
  350.6 6.5 collective-permute-start
  361.7 6.5 collective-permute-start
  372.8 6.5 collective-permute-start
  379.3 4.3 collective-permute-done
  385.1 6.5 collective-permute-start
  391.6 5.1 collective-permute-done
  398.1 6.5 collective-permute-start
  404.6 4.2 collective-permute-done
  410.3 6.5 collective-permute-start
  421.6 6.5 collective-permute-start
  432.7 6.5 collective-permute-start
  443.8 6.5 collective-permute-start
  457.5 15.4 %fusion.5 = f32[64,128,6]{2,1,0:T(8,128)} fusion(f32[6,6,1,64,128]{1,0,4,3,2:T(8,128)} %copy.143, f32[64,128,6]{2,1,0:T(8,128)} %copy.147), kind=kLoop, calls=%fused_computation.20 | loop fusion | flops 540672 | bytes 1572864
  479.0 194.8 %while.67 = (s32[]{:T(128)}, f32[6,64,128]{2,1,0:T(8,128)}, f32[6,6,64,128]{3,2,1,0:T(8,128)S(1)}, f32[6,64,128]{2,1,0:T(8,128)}, s32[]{:T(128)}) while((s32[]{:T(128)}, f32[6,64,128]{2,1,0:T(8,128)}, f32[6,6,64,128]{3,2,1,0:T(8,128)S(1)}, f32[6,64,128]{2,1,0:T(8,128)}, s32[]{:T(128)}) %tuple.132), condition=%wide.region_5.7_spmd, body=%wide.region_4.6_spmd.sunk | while | flops 589826 | bytes 2949221 | solution.py:104
  483.6 8.5 %collective-permute-done.1 = f32[6,64,128]{2,1,0:T(8,128)} collective-permute-done((f32[6,64,128]{2,1,0:T(8,128)}, f32[6,64,128]{2,1,0:T(8,128)}, u32[]{:S(2)}, u32[]{:S(2)}) %collective-permute-start.1) | collective-permute-done | bytes 196640 | tf_op jit(solution)/shard_map/while/body/eval_jaxpr/ppermute | solution.py:29
  496.7 8.1 %collective-permute-done.1 = f32[6,64,128]{2,1,0:T(8,128)} collective-permute-done((f32[6,64,128]{2,1,0:T(8,128)}, f32[6,64,128]{2,1,0:T(8,128)}, u32[]{:S(2)}, u32[]{:S(2)}) %collective-permute-start.1) | collective-permute-done | bytes 196640 | tf_op jit(solution)/shard_map/while/body/eval_jaxpr/ppermute | solution.py:29
  509.4 8.1 %collective-permute-done.1 = f32[6,64,128]{2,1,0:T(8,128)} collective-permute-done((f32[6,64,128]{2,1,0:T(8,128)}, f32[6,64,128]{2,1,0:T(8,128)}, u32[]{:S(2)}, u32[]{:S(2)}) %collective-permute-start.1) | collective-permute-done | bytes 196640 | tf_op jit(solution)/shard_map/while/body/eval_jaxpr/ppermute | solution.py:29
  522.1 8.1 %collective-permute-done.1 = f32[6,64,128]{2,1,0:T(8,128)} collective-permute-done((f32[6,64,128]{2,1,0:T(8,128)}, f32[6,64,128]{2,1,0:T(8,128)}, u32[]{:S(2)}, u32[]{:S(2)}) %collective-permute-start.1) | collective-permute-done | bytes 196640 | tf_op jit(solution)/shard_map/while/body/eval_jaxpr/ppermute | solution.py:29
  534.8 8.1 %collective-permute-done.1 = f32[6,64,128]{2,1,0:T(8,128)} collective-permute-done((f32[6,64,128]{2,1,0:T(8,128)}, f32[6,64,128]{2,1,0:T(8,128)}, u32[]{:S(2)}, u32[]{:S(2)}) %collective-permute-start.1) | collective-permute-done | bytes 196640 | tf_op jit(solution)/shard_map/while/body/eval_jaxpr/ppermute | solution.py:29
  547.4 8.8 %collective-permute-done.1 = f32[6,64,128]{2,1,0:T(8,128)} collective-permute-done((f32[6,64,128]{2,1,0:T(8,128)}, f32[6,64,128]{2,1,0:T(8,128)}, u32[]{:S(2)}, u32[]{:S(2)}) %collective-permute-start.1) | collective-permute-done | bytes 196640 | tf_op jit(solution)/shard_map/while/body/eval_jaxpr/ppermute | solution.py:29
  560.8 9.9 %collective-permute-done.1 = f32[6,64,128]{2,1,0:T(8,128)} collective-permute-done((f32[6,64,128]{2,1,0:T(8,128)}, f32[6,64,128]{2,1,0:T(8,128)}, u32[]{:S(2)}, u32[]{:S(2)}) %collective-permute-start.1) | collective-permute-done | bytes 196640 | tf_op jit(solution)/shard_map/while/body/eval_jaxpr/ppermute | solution.py:29
  575.3 9.3 %collective-permute-done.1 = f32[6,64,128]{2,1,0:T(8,128)} collective-permute-done((f32[6,64,128]{2,1,0:T(8,128)}, f32[6,64,128]{2,1,0:T(8,128)}, u32[]{:S(2)}, u32[]{:S(2)}) %collective-permute-start.1) | collective-permute-done | bytes 196640 | tf_op jit(solution)/shard_map/while/body/eval_jaxpr/ppermute | solution.py:29
  589.3 8.5 %collective-permute-done.1 = f32[6,64,128]{2,1,0:T(8,128)} collective-permute-done((f32[6,64,128]{2,1,0:T(8,128)}, f32[6,64,128]{2,1,0:T(8,128)}, u32[]{:S(2)}, u32[]{:S(2)}) %collective-permute-start.1) | collective-permute-done | bytes 196640 | tf_op jit(solution)/shard_map/while/body/eval_jaxpr/ppermute | solution.py:29
  602.3 8.1 %collective-permute-done.1 = f32[6,64,128]{2,1,0:T(8,128)} collective-permute-done((f32[6,64,128]{2,1,0:T(8,128)}, f32[6,64,128]{2,1,0:T(8,128)}, u32[]{:S(2)}, u32[]{:S(2)}) %collective-permute-start.1) | collective-permute-done | bytes 196640 | tf_op jit(solution)/shard_map/while/body/eval_jaxpr/ppermute | solution.py:29
  615.0 8.1 %collective-permute-done.1 = f32[6,64,128]{2,1,0:T(8,128)} collective-permute-done((f32[6,64,128]{2,1,0:T(8,128)}, f32[6,64,128]{2,1,0:T(8,128)}, u32[]{:S(2)}, u32[]{:S(2)}) %collective-permute-start.1) | collective-permute-done | bytes 196640 | tf_op jit(solution)/shard_map/while/body/eval_jaxpr/ppermute | solution.py:29
  627.7 8.1 %collective-permute-done.1 = f32[6,64,128]{2,1,0:T(8,128)} collective-permute-done((f32[6,64,128]{2,1,0:T(8,128)}, f32[6,64,128]{2,1,0:T(8,128)}, u32[]{:S(2)}, u32[]{:S(2)}) %collective-permute-start.1) | collective-permute-done | bytes 196640 | tf_op jit(solution)/shard_map/while/body/eval_jaxpr/ppermute | solution.py:29
  640.3 8.1 %collective-permute-done.1 = f32[6,64,128]{2,1,0:T(8,128)} collective-permute-done((f32[6,64,128]{2,1,0:T(8,128)}, f32[6,64,128]{2,1,0:T(8,128)}, u32[]{:S(2)}, u32[]{:S(2)}) %collective-permute-start.1) | collective-permute-done | bytes 196640 | tf_op jit(solution)/shard_map/while/body/eval_jaxpr/ppermute | solution.py:29
  653.0 8.1 %collective-permute-done.1 = f32[6,64,128]{2,1,0:T(8,128)} collective-permute-done((f32[6,64,128]{2,1,0:T(8,128)}, f32[6,64,128]{2,1,0:T(8,128)}, u32[]{:S(2)}, u32[]{:S(2)}) %collective-permute-start.1) | collective-permute-done | bytes 196640 | tf_op jit(solution)/shard_map/while/body/eval_jaxpr/ppermute | solution.py:29
  665.7 8.1 %collective-permute-done.1 = f32[6,64,128]{2,1,0:T(8,128)} collective-permute-done((f32[6,64,128]{2,1,0:T(8,128)}, f32[6,64,128]{2,1,0:T(8,128)}, u32[]{:S(2)}, u32[]{:S(2)}) %collective-permute-start.1) | collective-permute-done | bytes 196640 | tf_op jit(solution)/shard_map/while/body/eval_jaxpr/ppermute | solution.py:29
  673.8 5.4 while.68
  (156 shorter events, 177.4 us)
Async XLA Ops:
  0.0 30.7 %copy-start = (f32[6,6,2,64,128]{4,3,2,1,0:T(8,128)S(1)}, f32[6,6,2,64,128]{4,3,2,1,0:T(8,128)}, u32[]{:S(2)}) copy-start(f32[6,6,2,64,128]{4,3,2,1,0:T(8,128)} %param.21) | copy-start | bytes 7077892
  2.5 224.2 %collective-permute-start.4 = (f32[6,2,64,1]{3,0,2,1:T(8,128)}, f32[6,2,64,1]{3,0,2,1:T(8,128)S(1)}, u32[]{:S(2)}, u32[]{:S(2)}) collective-permute-start(f32[6,2,64,1]{3,0,2,1:T(8,128)} %get-tuple-element.441), channel_id=1, source_target_pairs={{1,0},{3,2},{5,4},{7,6},{9,8},{11,10},{13,12},{15,14},{17,16},{19,... | collective-permute-start | bytes 9224 | tf_op jit(solution)/shard_map/ppermute | solution.py:15
  3.8 222.9 %collective-permute-start.5 = (f32[6,2,64,1]{3,0,2,1:T(8,128)}, f32[6,2,64,1]{3,0,2,1:T(8,128)}, u32[]{:S(2)}, u32[]{:S(2)}) collective-permute-start(f32[6,2,64,1]{3,0,2,1:T(8,128)} %get-tuple-element.442), channel_id=1, source_target_pairs={{0,1},{2,3},{4,5},{6,7},{8,9},{10,11},{12,13},{14,15},{16,17},{18,... | collective-permute-start | bytes 9224 | tf_op jit(solution)/shard_map/ppermute | solution.py:14
  9.2 217.5 %collective-permute-start.2 = (f32[6,2,1,128]{3,0,2,1:T(8,128)S(1)}, f32[6,2,1,128]{3,0,2,1:T(8,128)S(1)}, u32[]{:S(2)}, u32[]{:S(2)}) collective-permute-start(f32[6,2,1,128]{3,0,2,1:T(8,128)S(1)} %get-tuple-element.439), channel_id=1, source_target_pairs={{2,0},{4,2},{6,4},{0,6},{3,1},{5,3},{7,5},{1,7},{10,8},{12,10},{14... | collective-permute-start | bytes 18440 | tf_op jit(solution)/shard_map/ppermute | solution.py:15
  29.1 200.2 %collective-permute-start.6 = (f32[6,256,128]{2,1,0:T(8,128)}, f32[6,256,128]{2,1,0:T(8,128)}, u32[]{:S(2)}, u32[]{:S(2)}) collective-permute-start(f32[6,256,128]{2,1,0:T(8,128)} %bitcast.127), channel_id=1, source_target_pairs={{120,0},{0,8},{8,16},{16,24},{24,32},{32,40},{40,48},{48,56},{56,6... | collective-permute-start | bytes 2359304 | tf_op jit(solution)/shard_map/ppermute | solution.py:23
  133.8 61.7 %copy-start.8 = (s32[1,64]{1,0:T(1,128)S(1)}, s32[1,64]{1,0:T(1,128)}, u32[]{:S(2)}) copy-start(s32[1,64]{1,0:T(1,128)} %param.22) | copy-start | bytes 772
  133.8 61.8 %copy-start.7 = (f32[64]{0:T(128)S(1)}, f32[64]{0:T(128)}, u32[]{:S(2)}) copy-start(f32[64]{0:T(128)} %param.23) | copy-start | bytes 772
  195.5 32.0 %collective-permute-start.3 = (f32[6,2,1,128]{3,0,2,1:T(8,128)S(1)}, f32[6,2,1,128]{3,0,2,1:T(8,128)S(1)}, u32[]{:S(2)}, u32[]{:S(2)}) collective-permute-start(f32[6,2,1,128]{3,0,2,1:T(8,128)S(1)} %get-tuple-element.440), channel_id=1, source_target_pairs={{0,2},{2,4},{4,6},{6,0},{1,3},{3,5},{5,7},{7,1},{8,10},{10,12},{12... | collective-permute-start | bytes 18440 | tf_op jit(solution)/shard_map/ppermute | solution.py:14
  211.3 16.2 %copy-start.6 = (f32[2,64,128]{2,1,0:T(8,128)S(1)}, f32[2,64,128]{2,1,0:T(8,128)}, u32[]{:S(2)}) copy-start(f32[2,64,128]{2,1,0:T(8,128)} %param.20) | copy-start | bytes 196612
  226.7 0.8 copy-start.4
  237.6 18.0 %copy-start.2 = (f32[6,2,64,128]{3,0,2,1:T(8,128)}, f32[6,2,64,128]{3,0,2,1:T(8,128)S(1)}, u32[]{:S(2)}) copy-start(f32[6,2,64,128]{3,0,2,1:T(8,128)S(1)} %get-tuple-element.433) | copy-start | bytes 1179652
  284.4 9.3 %collective-permute-start = (f32[6,64,128]{2,1,0:T(8,128)S(1)}, f32[6,64,128]{2,1,0:T(8,128)S(1)}, u32[]{:S(2)}, u32[]{:S(2)}) collective-permute-start(f32[6,64,128]{2,1,0:T(8,128)S(1)} %bitcast_add_fusion.8), channel_id=1, source_target_pairs={{0,8},{8,16},{16,24},{24,32},{32,40},{40,48},{48,56},{56,64},{64,7... | collective-permute-start | bytes 589832 | tf_op jit(solution)/shard_map/while/body/eval_jaxpr/ppermute | solution.py:29
  295.1 9.6 %collective-permute-start = (f32[6,64,128]{2,1,0:T(8,128)S(1)}, f32[6,64,128]{2,1,0:T(8,128)S(1)}, u32[]{:S(2)}, u32[]{:S(2)}) collective-permute-start(f32[6,64,128]{2,1,0:T(8,128)S(1)} %bitcast_add_fusion.8), channel_id=1, source_target_pairs={{0,8},{8,16},{16,24},{24,32},{32,40},{40,48},{48,56},{56,64},{64,7... | collective-permute-start | bytes 589832 | tf_op jit(solution)/shard_map/while/body/eval_jaxpr/ppermute | solution.py:29
  306.1 9.7 %collective-permute-start = (f32[6,64,128]{2,1,0:T(8,128)S(1)}, f32[6,64,128]{2,1,0:T(8,128)S(1)}, u32[]{:S(2)}, u32[]{:S(2)}) collective-permute-start(f32[6,64,128]{2,1,0:T(8,128)S(1)} %bitcast_add_fusion.8), channel_id=1, source_target_pairs={{0,8},{8,16},{16,24},{24,32},{32,40},{40,48},{48,56},{56,64},{64,7... | collective-permute-start | bytes 589832 | tf_op jit(solution)/shard_map/while/body/eval_jaxpr/ppermute | solution.py:29
  317.2 9.7 %collective-permute-start = (f32[6,64,128]{2,1,0:T(8,128)S(1)}, f32[6,64,128]{2,1,0:T(8,128)S(1)}, u32[]{:S(2)}, u32[]{:S(2)}) collective-permute-start(f32[6,64,128]{2,1,0:T(8,128)S(1)} %bitcast_add_fusion.8), channel_id=1, source_target_pairs={{0,8},{8,16},{16,24},{24,32},{32,40},{40,48},{48,56},{56,64},{64,7... | collective-permute-start | bytes 589832 | tf_op jit(solution)/shard_map/while/body/eval_jaxpr/ppermute | solution.py:29
  328.4 9.7 %collective-permute-start = (f32[6,64,128]{2,1,0:T(8,128)S(1)}, f32[6,64,128]{2,1,0:T(8,128)S(1)}, u32[]{:S(2)}, u32[]{:S(2)}) collective-permute-start(f32[6,64,128]{2,1,0:T(8,128)S(1)} %bitcast_add_fusion.8), channel_id=1, source_target_pairs={{0,8},{8,16},{16,24},{24,32},{32,40},{40,48},{48,56},{56,64},{64,7... | collective-permute-start | bytes 589832 | tf_op jit(solution)/shard_map/while/body/eval_jaxpr/ppermute | solution.py:29
  339.5 9.7 %collective-permute-start = (f32[6,64,128]{2,1,0:T(8,128)S(1)}, f32[6,64,128]{2,1,0:T(8,128)S(1)}, u32[]{:S(2)}, u32[]{:S(2)}) collective-permute-start(f32[6,64,128]{2,1,0:T(8,128)S(1)} %bitcast_add_fusion.8), channel_id=1, source_target_pairs={{0,8},{8,16},{16,24},{24,32},{32,40},{40,48},{48,56},{56,64},{64,7... | collective-permute-start | bytes 589832 | tf_op jit(solution)/shard_map/while/body/eval_jaxpr/ppermute | solution.py:29
  350.6 9.7 %collective-permute-start = (f32[6,64,128]{2,1,0:T(8,128)S(1)}, f32[6,64,128]{2,1,0:T(8,128)S(1)}, u32[]{:S(2)}, u32[]{:S(2)}) collective-permute-start(f32[6,64,128]{2,1,0:T(8,128)S(1)} %bitcast_add_fusion.8), channel_id=1, source_target_pairs={{0,8},{8,16},{16,24},{24,32},{32,40},{40,48},{48,56},{56,64},{64,7... | collective-permute-start | bytes 589832 | tf_op jit(solution)/shard_map/while/body/eval_jaxpr/ppermute | solution.py:29
  361.7 9.7 %collective-permute-start = (f32[6,64,128]{2,1,0:T(8,128)S(1)}, f32[6,64,128]{2,1,0:T(8,128)S(1)}, u32[]{:S(2)}, u32[]{:S(2)}) collective-permute-start(f32[6,64,128]{2,1,0:T(8,128)S(1)} %bitcast_add_fusion.8), channel_id=1, source_target_pairs={{0,8},{8,16},{16,24},{24,32},{32,40},{40,48},{48,56},{56,64},{64,7... | collective-permute-start | bytes 589832 | tf_op jit(solution)/shard_map/while/body/eval_jaxpr/ppermute | solution.py:29
  372.8 10.8 %collective-permute-start = (f32[6,64,128]{2,1,0:T(8,128)S(1)}, f32[6,64,128]{2,1,0:T(8,128)S(1)}, u32[]{:S(2)}, u32[]{:S(2)}) collective-permute-start(f32[6,64,128]{2,1,0:T(8,128)S(1)} %bitcast_add_fusion.8), channel_id=1, source_target_pairs={{0,8},{8,16},{16,24},{24,32},{32,40},{40,48},{48,56},{56,64},{64,7... | collective-permute-start | bytes 589832 | tf_op jit(solution)/shard_map/while/body/eval_jaxpr/ppermute | solution.py:29
  385.1 11.6 %collective-permute-start = (f32[6,64,128]{2,1,0:T(8,128)S(1)}, f32[6,64,128]{2,1,0:T(8,128)S(1)}, u32[]{:S(2)}, u32[]{:S(2)}) collective-permute-start(f32[6,64,128]{2,1,0:T(8,128)S(1)} %bitcast_add_fusion.8), channel_id=1, source_target_pairs={{0,8},{8,16},{16,24},{24,32},{32,40},{40,48},{48,56},{56,64},{64,7... | collective-permute-start | bytes 589832 | tf_op jit(solution)/shard_map/while/body/eval_jaxpr/ppermute | solution.py:29
  398.1 10.7 %collective-permute-start = (f32[6,64,128]{2,1,0:T(8,128)S(1)}, f32[6,64,128]{2,1,0:T(8,128)S(1)}, u32[]{:S(2)}, u32[]{:S(2)}) collective-permute-start(f32[6,64,128]{2,1,0:T(8,128)S(1)} %bitcast_add_fusion.8), channel_id=1, source_target_pairs={{0,8},{8,16},{16,24},{24,32},{32,40},{40,48},{48,56},{56,64},{64,7... | collective-permute-start | bytes 589832 | tf_op jit(solution)/shard_map/while/body/eval_jaxpr/ppermute | solution.py:29
  410.3 9.9 %collective-permute-start = (f32[6,64,128]{2,1,0:T(8,128)S(1)}, f32[6,64,128]{2,1,0:T(8,128)S(1)}, u32[]{:S(2)}, u32[]{:S(2)}) collective-permute-start(f32[6,64,128]{2,1,0:T(8,128)S(1)} %bitcast_add_fusion.8), channel_id=1, source_target_pairs={{0,8},{8,16},{16,24},{24,32},{32,40},{40,48},{48,56},{56,64},{64,7... | collective-permute-start | bytes 589832 | tf_op jit(solution)/shard_map/while/body/eval_jaxpr/ppermute | solution.py:29
  421.6 9.7 %collective-permute-start = (f32[6,64,128]{2,1,0:T(8,128)S(1)}, f32[6,64,128]{2,1,0:T(8,128)S(1)}, u32[]{:S(2)}, u32[]{:S(2)}) collective-permute-start(f32[6,64,128]{2,1,0:T(8,128)S(1)} %bitcast_add_fusion.8), channel_id=1, source_target_pairs={{0,8},{8,16},{16,24},{24,32},{32,40},{40,48},{48,56},{56,64},{64,7... | collective-permute-start | bytes 589832 | tf_op jit(solution)/shard_map/while/body/eval_jaxpr/ppermute | solution.py:29
  432.7 9.7 %collective-permute-start = (f32[6,64,128]{2,1,0:T(8,128)S(1)}, f32[6,64,128]{2,1,0:T(8,128)S(1)}, u32[]{:S(2)}, u32[]{:S(2)}) collective-permute-start(f32[6,64,128]{2,1,0:T(8,128)S(1)} %bitcast_add_fusion.8), channel_id=1, source_target_pairs={{0,8},{8,16},{16,24},{24,32},{32,40},{40,48},{48,56},{56,64},{64,7... | collective-permute-start | bytes 589832 | tf_op jit(solution)/shard_map/while/body/eval_jaxpr/ppermute | solution.py:29
  443.8 9.7 %collective-permute-start = (f32[6,64,128]{2,1,0:T(8,128)S(1)}, f32[6,64,128]{2,1,0:T(8,128)S(1)}, u32[]{:S(2)}, u32[]{:S(2)}) collective-permute-start(f32[6,64,128]{2,1,0:T(8,128)S(1)} %bitcast_add_fusion.8), channel_id=1, source_target_pairs={{0,8},{8,16},{16,24},{24,32},{32,40},{40,48},{48,56},{56,64},{64,7... | collective-permute-start | bytes 589832 | tf_op jit(solution)/shard_map/while/body/eval_jaxpr/ppermute | solution.py:29
  454.0 3.6 copy-start.3
  473.0 6.0 copy-start.1
  481.7 10.4 %collective-permute-start.1 = (f32[6,64,128]{2,1,0:T(8,128)}, f32[6,64,128]{2,1,0:T(8,128)}, u32[]{:S(2)}, u32[]{:S(2)}) collective-permute-start(f32[6,64,128]{2,1,0:T(8,128)} %bitcast_add_fusion.9), channel_id=1, source_target_pairs={{8,0},{16,8},{24,16},{32,24},{40,32},{48,40},{56,48},{64,56},{72,6... | collective-permute-start | bytes 589832 | tf_op jit(solution)/shard_map/while/body/eval_jaxpr/ppermute | solution.py:29
  494.8 10.0 %collective-permute-start.1 = (f32[6,64,128]{2,1,0:T(8,128)}, f32[6,64,128]{2,1,0:T(8,128)}, u32[]{:S(2)}, u32[]{:S(2)}) collective-permute-start(f32[6,64,128]{2,1,0:T(8,128)} %bitcast_add_fusion.9), channel_id=1, source_target_pairs={{8,0},{16,8},{24,16},{32,24},{40,32},{48,40},{56,48},{64,56},{72,6... | collective-permute-start | bytes 589832 | tf_op jit(solution)/shard_map/while/body/eval_jaxpr/ppermute | solution.py:29
  507.5 10.0 %collective-permute-start.1 = (f32[6,64,128]{2,1,0:T(8,128)}, f32[6,64,128]{2,1,0:T(8,128)}, u32[]{:S(2)}, u32[]{:S(2)}) collective-permute-start(f32[6,64,128]{2,1,0:T(8,128)} %bitcast_add_fusion.9), channel_id=1, source_target_pairs={{8,0},{16,8},{24,16},{32,24},{40,32},{48,40},{56,48},{64,56},{72,6... | collective-permute-start | bytes 589832 | tf_op jit(solution)/shard_map/while/body/eval_jaxpr/ppermute | solution.py:29
  520.2 10.0 %collective-permute-start.1 = (f32[6,64,128]{2,1,0:T(8,128)}, f32[6,64,128]{2,1,0:T(8,128)}, u32[]{:S(2)}, u32[]{:S(2)}) collective-permute-start(f32[6,64,128]{2,1,0:T(8,128)} %bitcast_add_fusion.9), channel_id=1, source_target_pairs={{8,0},{16,8},{24,16},{32,24},{40,32},{48,40},{56,48},{64,56},{72,6... | collective-permute-start | bytes 589832 | tf_op jit(solution)/shard_map/while/body/eval_jaxpr/ppermute | solution.py:29
  532.8 10.0 %collective-permute-start.1 = (f32[6,64,128]{2,1,0:T(8,128)}, f32[6,64,128]{2,1,0:T(8,128)}, u32[]{:S(2)}, u32[]{:S(2)}) collective-permute-start(f32[6,64,128]{2,1,0:T(8,128)} %bitcast_add_fusion.9), channel_id=1, source_target_pairs={{8,0},{16,8},{24,16},{32,24},{40,32},{48,40},{56,48},{64,56},{72,6... | collective-permute-start | bytes 589832 | tf_op jit(solution)/shard_map/while/body/eval_jaxpr/ppermute | solution.py:29
  545.5 10.7 %collective-permute-start.1 = (f32[6,64,128]{2,1,0:T(8,128)}, f32[6,64,128]{2,1,0:T(8,128)}, u32[]{:S(2)}, u32[]{:S(2)}) collective-permute-start(f32[6,64,128]{2,1,0:T(8,128)} %bitcast_add_fusion.9), channel_id=1, source_target_pairs={{8,0},{16,8},{24,16},{32,24},{40,32},{48,40},{56,48},{64,56},{72,6... | collective-permute-start | bytes 589832 | tf_op jit(solution)/shard_map/while/body/eval_jaxpr/ppermute | solution.py:29
  558.9 11.8 %collective-permute-start.1 = (f32[6,64,128]{2,1,0:T(8,128)}, f32[6,64,128]{2,1,0:T(8,128)}, u32[]{:S(2)}, u32[]{:S(2)}) collective-permute-start(f32[6,64,128]{2,1,0:T(8,128)} %bitcast_add_fusion.9), channel_id=1, source_target_pairs={{8,0},{16,8},{24,16},{32,24},{40,32},{48,40},{56,48},{64,56},{72,6... | collective-permute-start | bytes 589832 | tf_op jit(solution)/shard_map/while/body/eval_jaxpr/ppermute | solution.py:29
  573.4 11.2 %collective-permute-start.1 = (f32[6,64,128]{2,1,0:T(8,128)}, f32[6,64,128]{2,1,0:T(8,128)}, u32[]{:S(2)}, u32[]{:S(2)}) collective-permute-start(f32[6,64,128]{2,1,0:T(8,128)} %bitcast_add_fusion.9), channel_id=1, source_target_pairs={{8,0},{16,8},{24,16},{32,24},{40,32},{48,40},{56,48},{64,56},{72,6... | collective-permute-start | bytes 589832 | tf_op jit(solution)/shard_map/while/body/eval_jaxpr/ppermute | solution.py:29
  587.3 10.4 %collective-permute-start.1 = (f32[6,64,128]{2,1,0:T(8,128)}, f32[6,64,128]{2,1,0:T(8,128)}, u32[]{:S(2)}, u32[]{:S(2)}) collective-permute-start(f32[6,64,128]{2,1,0:T(8,128)} %bitcast_add_fusion.9), channel_id=1, source_target_pairs={{8,0},{16,8},{24,16},{32,24},{40,32},{48,40},{56,48},{64,56},{72,6... | collective-permute-start | bytes 589832 | tf_op jit(solution)/shard_map/while/body/eval_jaxpr/ppermute | solution.py:29
  600.4 10.0 %collective-permute-start.1 = (f32[6,64,128]{2,1,0:T(8,128)}, f32[6,64,128]{2,1,0:T(8,128)}, u32[]{:S(2)}, u32[]{:S(2)}) collective-permute-start(f32[6,64,128]{2,1,0:T(8,128)} %bitcast_add_fusion.9), channel_id=1, source_target_pairs={{8,0},{16,8},{24,16},{32,24},{40,32},{48,40},{56,48},{64,56},{72,6... | collective-permute-start | bytes 589832 | tf_op jit(solution)/shard_map/while/body/eval_jaxpr/ppermute | solution.py:29
  613.1 10.0 %collective-permute-start.1 = (f32[6,64,128]{2,1,0:T(8,128)}, f32[6,64,128]{2,1,0:T(8,128)}, u32[]{:S(2)}, u32[]{:S(2)}) collective-permute-start(f32[6,64,128]{2,1,0:T(8,128)} %bitcast_add_fusion.9), channel_id=1, source_target_pairs={{8,0},{16,8},{24,16},{32,24},{40,32},{48,40},{56,48},{64,56},{72,6... | collective-permute-start | bytes 589832 | tf_op jit(solution)/shard_map/while/body/eval_jaxpr/ppermute | solution.py:29
  625.7 10.0 %collective-permute-start.1 = (f32[6,64,128]{2,1,0:T(8,128)}, f32[6,64,128]{2,1,0:T(8,128)}, u32[]{:S(2)}, u32[]{:S(2)}) collective-permute-start(f32[6,64,128]{2,1,0:T(8,128)} %bitcast_add_fusion.9), channel_id=1, source_target_pairs={{8,0},{16,8},{24,16},{32,24},{40,32},{48,40},{56,48},{64,56},{72,6... | collective-permute-start | bytes 589832 | tf_op jit(solution)/shard_map/while/body/eval_jaxpr/ppermute | solution.py:29
  638.4 10.0 %collective-permute-start.1 = (f32[6,64,128]{2,1,0:T(8,128)}, f32[6,64,128]{2,1,0:T(8,128)}, u32[]{:S(2)}, u32[]{:S(2)}) collective-permute-start(f32[6,64,128]{2,1,0:T(8,128)} %bitcast_add_fusion.9), channel_id=1, source_target_pairs={{8,0},{16,8},{24,16},{32,24},{40,32},{48,40},{56,48},{64,56},{72,6... | collective-permute-start | bytes 589832 | tf_op jit(solution)/shard_map/while/body/eval_jaxpr/ppermute | solution.py:29
  651.1 10.0 %collective-permute-start.1 = (f32[6,64,128]{2,1,0:T(8,128)}, f32[6,64,128]{2,1,0:T(8,128)}, u32[]{:S(2)}, u32[]{:S(2)}) collective-permute-start(f32[6,64,128]{2,1,0:T(8,128)} %bitcast_add_fusion.9), channel_id=1, source_target_pairs={{8,0},{16,8},{24,16},{32,24},{40,32},{48,40},{56,48},{64,56},{72,6... | collective-permute-start | bytes 589832 | tf_op jit(solution)/shard_map/while/body/eval_jaxpr/ppermute | solution.py:29
  663.8 10.0 %collective-permute-start.1 = (f32[6,64,128]{2,1,0:T(8,128)}, f32[6,64,128]{2,1,0:T(8,128)}, u32[]{:S(2)}, u32[]{:S(2)}) collective-permute-start(f32[6,64,128]{2,1,0:T(8,128)} %bitcast_add_fusion.9), channel_id=1, source_target_pairs={{8,0},{16,8},{24,16},{32,24},{40,32},{48,40},{56,48},{64,56},{72,6... | collective-permute-start | bytes 589832 | tf_op jit(solution)/shard_map/while/body/eval_jaxpr/ppermute | solution.py:29
  679.2 0.7 copy-start.5
where the time goes:
time: 683 us; the launch traced here: 680 us
  waiting for transfers between devices  181 us (27%)
  matrix products  134 us (20%)
  starting transfers between devices  133 us (19%)
  other arithmetic  121 us (18%)
  local copies, waits for them, and re-layouts  95.5 us (14%)
  blocking collectives  15.9 us (2%)
    ppermute x30, waiting for transfers between devices, shifted(): return lax.ppermute(block, axis, route)  181 us
    dot_general x2, matrix products, compose(): jnp.einsum('ab...,bc...->ac...', later, earlier, precision=lax.Precision....  134 us
    ppermute x30, starting transfers between devices, shifted(): return lax.ppermute(block, axis, route)  122 us
    unnamed x4, other arithmetic  48.5 us
    unnamed x26, local copies, waits for them, and re-layouts  40.9 us
    dot_general x34, other arithmetic, apply_block(): jnp.einsum('ab...,b...->a...', matrix, vector, precision=lax.Precision.HI...  39.4 us
    add x15, other arithmetic, upper_pass(): leaving = apply_block(upper_maps[0], incoming) + upper_maps[1]  24.4 us
    all_gather x1, blocking collectives, on_device(): annulus = lax.all_gather(face, 'passage', axis=1, tiled=True)  15.9 us
  transfers between devices with their start and end apart: 35, of which 30 were waited for; matrix products, arithmetic and copies ran while one was open for 29% of the time, Pallas kernels for 0%

commit v1 on v0

--- a/solution.py
+++ b/solution.py
@@ -50,7 +50,9 @@
     )
     source = residual - lateral_coef[None] * neighbours
     face = dq_old[:, planes - 1]
-    annulus = lax.all_gather(face, "passage", axis=1, tiled=True)
+    annulus = jnp.concatenate(
+        lax.all_to_all(jnp.stack([face] * lax.axis_size("passage")), "passage", 0, 0), axis=1
+    )
     upstream = passed_along(annulus, "stream", 1)
     total = upstream.shape[1]
     donors = match_list[0]

time: 683 us -> 676 us (0.990)
  blocking collectives: 15.9 us -> 0 us
    all_gather x1 -> x0, blocking collectives: 15.9 us -> none  [on_device(): annulus = lax.all_gather(face, 'passage', axis=1, tiled=True)]
    unnamed x26 -> x25, local copies, waits for them, and re-layouts: 40.9 us -> 40.8 us
  transfers between devices with their start and end apart: 35 -> 36, of which waited for: 30 -> 30; matrix products, arithmetic and copies ran while one was open for 29% -> 30% of each run, Pallas kernels for 0% -> 0%
where the time goes in v1:
time: 676 us; the launch traced here: 673 us
  waiting for transfers between devices  183 us (27%)
  starting transfers between devices  137 us (20%)
  matrix products  134 us (20%)
  other arithmetic  121 us (18%)
  local copies, waits for them, and re-layouts  97.6 us (14%)
    ppermute x30, waiting for transfers between devices, shifted(): return lax.ppermute(block, axis, route)  183 us
    dot_general x2, matrix products, compose(): jnp.einsum('ab...,bc...->ac...', later, earlier, precision=lax.Precision....  134 us
    ppermute x30, starting transfers between devices, shifted(): return lax.ppermute(block, axis, route)  122 us
    unnamed x4, other arithmetic  48.5 us
    unnamed x25, local copies, waits for them, and re-layouts  40.8 us
    dot_general x34, other arithmetic, apply_block(): jnp.einsum('ab...,b...->a...', matrix, vector, precision=lax.Precision.HI...  39.4 us
    add x15, other arithmetic, upper_pass(): leaving = apply_block(upper_maps[0], incoming) + upper_maps[1]  24.4 us
    while x1, local copies, waits for them, and re-layouts, on_device(): lax.fori_loop(0, blocks - 1, lower_pass, jnp.zeros_like(lower_maps[1]))  15.6 us
  transfers between devices with their start and end apart: 36, of which 30 were waited for; matrix products, arithmetic and copies ran while one was open for 30% of the time, Pallas kernels for 0%

profile of v1, /device:TPU:24, one launch (start us, length us, event | category | flops | bytes accessed | tf_op | source)
XLA Modules:
  0.0 672.7 jit_solution(7881667384796818001)
XLA Ops:
  3.8 5.4 collective-permute-start.5
  13.0 4.2 all-to-all-start
  18.8 14.8 %copy.120 = f32[6,6,1,64,128]{1,0,4,3,2:T(8,128)} copy(f32[6,6,1,64,128]{4,3,2,1,0:T(8,128)} %get-tuple-element.420) | data formatting | bytes 2359296
  33.6 15.0 %copy.119 = f32[6,6,1,64,128]{0,1,4,3,2:T(8,128)} copy(f32[6,6,1,64,128]{4,3,2,1,0:T(8,128)} %get-tuple-element.419) | data formatting | bytes 2359296
  48.6 71.8 %fusion.17 = f32[6,6,64,128]{0,1,3,2:T(8,128)} fusion(f32[6,6,1,64,128]{0,1,4,3,2:T(8,128)} %copy.119, f32[6,6,1,64,128]{1,0,4,3,2:T(8,128)} %copy.120), kind=kOutput, calls=%fused_computation.28 | convolution fusion | flops 21233664 | bytes 3538944 | tf_op jit(solution)/shard_map/while/body/eval_jaxpr/ab...,bc...->ac.../dot_general | solution.py:37
  120.4 61.7 %fusion.12 = f32[6,6,64,128]{0,1,3,2:T(8,128)} fusion(f32[6,6,1,64,128]{1,0,4,3,2:T(8,128)} %copy.120, f32[6,6,1,64,128]{0,1,4,3,2:T(8,128)} %copy.119), kind=kOutput, calls=%fused_computation.27 | convolution fusion | flops 21233664 | bytes 3538944 | tf_op jit(solution)/shard_map/while/body/eval_jaxpr/ab...,bc...->ac.../dot_general | solution.py:37
  186.1 15.6 %copy.59 = f32[6,6,64,128]{3,2,1,0:T(8,128)} copy(f32[6,6,64,128]{0,1,3,2:T(8,128)} %fusion.17) | data formatting | bytes 2359296 | tf_op jit(solution)/shard_map/while | solution.py:80
  201.7 15.4 %copy.62 = f32[6,6,64,128]{3,2,1,0:T(8,128)} copy(f32[6,6,64,128]{0,1,3,2:T(8,128)} %fusion.12) | data formatting | bytes 2359296 | tf_op jit(solution)/shard_map/while | solution.py:106
  230.7 15.3 %fusion.4 = f32[64,128,6]{2,1,0:T(8,128)} fusion(f32[6,6,1,64,128]{1,0,4,3,2:T(8,128)} %copy.120, f32[64,128,6]{2,1,0:T(8,128)} %copy.121), kind=kLoop, calls=%fused_computation.19 | loop fusion | flops 540672 | bytes 1572864
  253.7 16.8 %fusion.3 = f32[64,128,6]{2,1,0:T(8,128)} fusion(f32[6,6,1,64,128]{0,1,4,3,2:T(8,128)} %copy.119, f32[64,128,6]{2,1,0:T(8,128)} %copy.122), kind=kLoop, calls=%fused_computation.16 | loop fusion | flops 540672 | bytes 1572864
  273.4 172.3 %while.65 = (s32[]{:T(128)}, f32[6,64,128]{2,1,0:T(8,128)S(1)}, f32[6,6,64,128]{3,2,1,0:T(8,128)}, f32[6,64,128]{2,1,0:T(8,128)S(1)}, s32[]{:T(128)}) while((s32[]{:T(128)}, f32[6,64,128]{2,1,0:T(8,128)S(1)}, f32[6,6,64,128]{3,2,1,0:T(8,128)}, f32[6,64,128]{2,1,0:T(8,128)S(1)}, s32[]{:T(128)}) %tuple.129), condition=%wide.region_1.3_spmd, body=%wide.region_0.2_spmd.sunk | while | flops 589826 | bytes 2949221 | solution.py:80
  278.4 4.1 collective-permute-done
  283.9 5.6 collective-permute-start
  294.9 6.5 collective-permute-start
  301.4 5.1 collective-permute-done
  308.0 6.5 collective-permute-start
  314.5 4.4 collective-permute-done
  320.3 6.5 collective-permute-start
  331.8 6.5 collective-permute-start
  343.0 6.5 collective-permute-start
  354.1 6.5 collective-permute-start
  365.2 6.5 collective-permute-start
  376.3 6.5 collective-permute-start
  387.4 6.5 collective-permute-start
  399.0 6.5 collective-permute-start
  405.5 4.8 collective-permute-done
  411.7 6.5 collective-permute-start
  418.2 4.6 collective-permute-done
  424.3 6.5 collective-permute-start
  436.0 6.5 collective-permute-start
  449.7 15.4 %fusion.5 = f32[64,128,6]{2,1,0:T(8,128)} fusion(f32[6,6,1,64,128]{1,0,4,3,2:T(8,128)} %copy.120, f32[64,128,6]{2,1,0:T(8,128)} %copy.123), kind=kLoop, calls=%fused_computation.20 | loop fusion | flops 540672 | bytes 1572864
  471.2 195.3 %while.67 = (s32[]{:T(128)}, f32[6,64,128]{2,1,0:T(8,128)}, f32[6,6,64,128]{3,2,1,0:T(8,128)S(1)}, f32[6,64,128]{2,1,0:T(8,128)}, s32[]{:T(128)}) while((s32[]{:T(128)}, f32[6,64,128]{2,1,0:T(8,128)}, f32[6,6,64,128]{3,2,1,0:T(8,128)S(1)}, f32[6,64,128]{2,1,0:T(8,128)}, s32[]{:T(128)}) %tuple.128), condition=%wide.region_5.7_spmd, body=%wide.region_4.6_spmd.sunk | while | flops 589826 | bytes 2949221 | solution.py:106
  475.8 9.0 %collective-permute-done.1 = f32[6,64,128]{2,1,0:T(8,128)} collective-permute-done((f32[6,64,128]{2,1,0:T(8,128)}, f32[6,64,128]{2,1,0:T(8,128)}, u32[]{:S(2)}, u32[]{:S(2)}) %collective-permute-start.1) | collective-permute-done | bytes 196640 | tf_op jit(solution)/shard_map/while/body/eval_jaxpr/ppermute | solution.py:29
  489.4 8.1 %collective-permute-done.1 = f32[6,64,128]{2,1,0:T(8,128)} collective-permute-done((f32[6,64,128]{2,1,0:T(8,128)}, f32[6,64,128]{2,1,0:T(8,128)}, u32[]{:S(2)}, u32[]{:S(2)}) %collective-permute-start.1) | collective-permute-done | bytes 196640 | tf_op jit(solution)/shard_map/while/body/eval_jaxpr/ppermute | solution.py:29
  502.0 8.1 %collective-permute-done.1 = f32[6,64,128]{2,1,0:T(8,128)} collective-permute-done((f32[6,64,128]{2,1,0:T(8,128)}, f32[6,64,128]{2,1,0:T(8,128)}, u32[]{:S(2)}, u32[]{:S(2)}) %collective-permute-start.1) | collective-permute-done | bytes 196640 | tf_op jit(solution)/shard_map/while/body/eval_jaxpr/ppermute | solution.py:29
  514.7 8.1 %collective-permute-done.1 = f32[6,64,128]{2,1,0:T(8,128)} collective-permute-done((f32[6,64,128]{2,1,0:T(8,128)}, f32[6,64,128]{2,1,0:T(8,128)}, u32[]{:S(2)}, u32[]{:S(2)}) %collective-permute-start.1) | collective-permute-done | bytes 196640 | tf_op jit(solution)/shard_map/while/body/eval_jaxpr/ppermute | solution.py:29
  527.4 8.1 %collective-permute-done.1 = f32[6,64,128]{2,1,0:T(8,128)} collective-permute-done((f32[6,64,128]{2,1,0:T(8,128)}, f32[6,64,128]{2,1,0:T(8,128)}, u32[]{:S(2)}, u32[]{:S(2)}) %collective-permute-start.1) | collective-permute-done | bytes 196640 | tf_op jit(solution)/shard_map/while/body/eval_jaxpr/ppermute | solution.py:29
  540.1 8.1 %collective-permute-done.1 = f32[6,64,128]{2,1,0:T(8,128)} collective-permute-done((f32[6,64,128]{2,1,0:T(8,128)}, f32[6,64,128]{2,1,0:T(8,128)}, u32[]{:S(2)}, u32[]{:S(2)}) %collective-permute-start.1) | collective-permute-done | bytes 196640 | tf_op jit(solution)/shard_map/while/body/eval_jaxpr/ppermute | solution.py:29
  552.7 8.1 %collective-permute-done.1 = f32[6,64,128]{2,1,0:T(8,128)} collective-permute-done((f32[6,64,128]{2,1,0:T(8,128)}, f32[6,64,128]{2,1,0:T(8,128)}, u32[]{:S(2)}, u32[]{:S(2)}) %collective-permute-start.1) | collective-permute-done | bytes 196640 | tf_op jit(solution)/shard_map/while/body/eval_jaxpr/ppermute | solution.py:29
  565.4 8.1 %collective-permute-done.1 = f32[6,64,128]{2,1,0:T(8,128)} collective-permute-done((f32[6,64,128]{2,1,0:T(8,128)}, f32[6,64,128]{2,1,0:T(8,128)}, u32[]{:S(2)}, u32[]{:S(2)}) %collective-permute-start.1) | collective-permute-done | bytes 196640 | tf_op jit(solution)/shard_map/while/body/eval_jaxpr/ppermute | solution.py:29
  578.1 9.2 %collective-permute-done.1 = f32[6,64,128]{2,1,0:T(8,128)} collective-permute-done((f32[6,64,128]{2,1,0:T(8,128)}, f32[6,64,128]{2,1,0:T(8,128)}, u32[]{:S(2)}, u32[]{:S(2)}) %collective-permute-start.1) | collective-permute-done | bytes 196640 | tf_op jit(solution)/shard_map/while/body/eval_jaxpr/ppermute | solution.py:29
  591.9 10.0 %collective-permute-done.1 = f32[6,64,128]{2,1,0:T(8,128)} collective-permute-done((f32[6,64,128]{2,1,0:T(8,128)}, f32[6,64,128]{2,1,0:T(8,128)}, u32[]{:S(2)}, u32[]{:S(2)}) %collective-permute-start.1) | collective-permute-done | bytes 196640 | tf_op jit(solution)/shard_map/while/body/eval_jaxpr/ppermute | solution.py:29
  606.5 9.1 %collective-permute-done.1 = f32[6,64,128]{2,1,0:T(8,128)} collective-permute-done((f32[6,64,128]{2,1,0:T(8,128)}, f32[6,64,128]{2,1,0:T(8,128)}, u32[]{:S(2)}, u32[]{:S(2)}) %collective-permute-start.1) | collective-permute-done | bytes 196640 | tf_op jit(solution)/shard_map/while/body/eval_jaxpr/ppermute | solution.py:29
  620.2 8.3 %collective-permute-done.1 = f32[6,64,128]{2,1,0:T(8,128)} collective-permute-done((f32[6,64,128]{2,1,0:T(8,128)}, f32[6,64,128]{2,1,0:T(8,128)}, u32[]{:S(2)}, u32[]{:S(2)}) %collective-permute-start.1) | collective-permute-done | bytes 196640 | tf_op jit(solution)/shard_map/while/body/eval_jaxpr/ppermute | solution.py:29
  633.1 8.1 %collective-permute-done.1 = f32[6,64,128]{2,1,0:T(8,128)} collective-permute-done((f32[6,64,128]{2,1,0:T(8,128)}, f32[6,64,128]{2,1,0:T(8,128)}, u32[]{:S(2)}, u32[]{:S(2)}) %collective-permute-start.1) | collective-permute-done | bytes 196640 | tf_op jit(solution)/shard_map/while/body/eval_jaxpr/ppermute | solution.py:29
  645.8 8.1 %collective-permute-done.1 = f32[6,64,128]{2,1,0:T(8,128)} collective-permute-done((f32[6,64,128]{2,1,0:T(8,128)}, f32[6,64,128]{2,1,0:T(8,128)}, u32[]{:S(2)}, u32[]{:S(2)}) %collective-permute-start.1) | collective-permute-done | bytes 196640 | tf_op jit(solution)/shard_map/while/body/eval_jaxpr/ppermute | solution.py:29
  658.4 8.1 %collective-permute-done.1 = f32[6,64,128]{2,1,0:T(8,128)} collective-permute-done((f32[6,64,128]{2,1,0:T(8,128)}, f32[6,64,128]{2,1,0:T(8,128)}, u32[]{:S(2)}, u32[]{:S(2)}) %collective-permute-start.1) | collective-permute-done | bytes 196640 | tf_op jit(solution)/shard_map/while/body/eval_jaxpr/ppermute | solution.py:29
  666.5 5.4 while.68
  (157 shorter events, 181.6 us)
Async XLA Ops:
  0.0 17.2 %copy-start = (f32[6,6,2,64,128]{4,3,2,1,0:T(8,128)S(1)}, f32[6,6,2,64,128]{4,3,2,1,0:T(8,128)}, u32[]{:S(2)}) copy-start(f32[6,6,2,64,128]{4,3,2,1,0:T(8,128)} %param.21) | copy-start | bytes 7077892
  2.5 214.6 %collective-permute-start.4 = (f32[6,2,64,1]{3,0,2,1:T(8,128)}, f32[6,2,64,1]{3,0,2,1:T(8,128)S(1)}, u32[]{:S(2)}, u32[]{:S(2)}) collective-permute-start(f32[6,2,64,1]{3,0,2,1:T(8,128)} %get-tuple-element.423), channel_id=1, source_target_pairs={{1,0},{3,2},{5,4},{7,6},{9,8},{11,10},{13,12},{15,14},{17,16},{19,... | collective-permute-start | bytes 9224 | tf_op jit(solution)/shard_map/ppermute | solution.py:15
  3.8 213.4 %collective-permute-start.5 = (f32[6,2,64,1]{3,0,2,1:T(8,128)}, f32[6,2,64,1]{3,0,2,1:T(8,128)}, u32[]{:S(2)}, u32[]{:S(2)}) collective-permute-start(f32[6,2,64,1]{3,0,2,1:T(8,128)} %get-tuple-element.424), channel_id=1, source_target_pairs={{0,1},{2,3},{4,5},{6,7},{8,9},{10,11},{12,13},{14,15},{16,17},{18,... | collective-permute-start | bytes 9224 | tf_op jit(solution)/shard_map/ppermute | solution.py:14
  9.2 208.0 %collective-permute-start.2 = (f32[6,2,1,128]{3,0,2,1:T(8,128)S(1)}, f32[6,2,1,128]{3,0,2,1:T(8,128)S(1)}, u32[]{:S(2)}, u32[]{:S(2)}) collective-permute-start(f32[6,2,1,128]{3,0,2,1:T(8,128)S(1)} %get-tuple-element.421), channel_id=1, source_target_pairs={{2,0},{4,2},{6,4},{0,6},{3,1},{5,3},{7,5},{1,7},{10,8},{12,10},{14... | collective-permute-start | bytes 18440 | tf_op jit(solution)/shard_map/ppermute | solution.py:15
  13.0 169.1 %all-to-all-start = ((f32[4,6,64,128]{3,2,1,0:T(8,128)}), f32[4,6,64,128]{3,2,1,0:T(8,128)}, u32[]{:S(2)}, u32[]{:S(2)}) async-start(f32[4,6,64,128]{3,2,1,0:T(8,128)} %stack.3), calls=%async_computation | async-start | bytes 1572864 | tf_op jit(solution)/shard_map/all_to_all | solution.py:54
  120.4 61.7 %copy-start.8 = (s32[1,64]{1,0:T(1,128)S(1)}, s32[1,64]{1,0:T(1,128)}, u32[]{:S(2)}) copy-start(s32[1,64]{1,0:T(1,128)} %param.22) | copy-start | bytes 772
  120.4 65.5 %copy-start.7 = (f32[64]{0:T(128)S(1)}, f32[64]{0:T(128)}, u32[]{:S(2)}) copy-start(f32[64]{0:T(128)} %param.23) | copy-start | bytes 772
  184.3 35.5 %collective-permute-start.6 = (f32[6,256,128]{2,1,0:T(8,128)}, f32[6,256,128]{2,1,0:T(8,128)}, u32[]{:S(2)}, u32[]{:S(2)}) collective-permute-start(f32[6,256,128]{2,1,0:T(8,128)} %bitcast.33), channel_id=1, source_target_pairs={{120,0},{0,8},{8,16},{16,24},{24,32},{32,40},{40,48},{48,56},{56,6... | collective-permute-start | bytes 2359304 | tf_op jit(solution)/shard_map/ppermute | solution.py:23
  185.9 32.1 %collective-permute-start.3 = (f32[6,2,1,128]{3,0,2,1:T(8,128)S(1)}, f32[6,2,1,128]{3,0,2,1:T(8,128)S(1)}, u32[]{:S(2)}, u32[]{:S(2)}) collective-permute-start(f32[6,2,1,128]{3,0,2,1:T(8,128)S(1)} %get-tuple-element.422), channel_id=1, source_target_pairs={{0,2},{2,4},{4,6},{6,0},{1,3},{3,5},{5,7},{7,1},{8,10},{10,12},{12... | collective-permute-start | bytes 18440 | tf_op jit(solution)/shard_map/ppermute | solution.py:14
  201.7 16.2 %copy-start.6 = (f32[2,64,128]{2,1,0:T(8,128)S(1)}, f32[2,64,128]{2,1,0:T(8,128)}, u32[]{:S(2)}) copy-start(f32[2,64,128]{2,1,0:T(8,128)} %param.20) | copy-start | bytes 196612
  217.2 0.8 copy-start.4
  228.0 18.0 %copy-start.2 = (f32[6,2,64,128]{3,0,2,1:T(8,128)}, f32[6,2,64,128]{3,0,2,1:T(8,128)S(1)}, u32[]{:S(2)}) copy-start(f32[6,2,64,128]{3,0,2,1:T(8,128)S(1)} %get-tuple-element.415) | copy-start | bytes 1179652
  274.9 7.6 %collective-permute-start = (f32[6,64,128]{2,1,0:T(8,128)S(1)}, f32[6,64,128]{2,1,0:T(8,128)S(1)}, u32[]{:S(2)}, u32[]{:S(2)}) collective-permute-start(f32[6,64,128]{2,1,0:T(8,128)S(1)} %bitcast_add_fusion.8), channel_id=1, source_target_pairs={{0,8},{8,16},{16,24},{24,32},{32,40},{40,48},{48,56},{56,64},{64,7... | collective-permute-start | bytes 589832 | tf_op jit(solution)/shard_map/while/body/eval_jaxpr/ppermute | solution.py:29
  283.9 9.6 %collective-permute-start = (f32[6,64,128]{2,1,0:T(8,128)S(1)}, f32[6,64,128]{2,1,0:T(8,128)S(1)}, u32[]{:S(2)}, u32[]{:S(2)}) collective-permute-start(f32[6,64,128]{2,1,0:T(8,128)S(1)} %bitcast_add_fusion.8), channel_id=1, source_target_pairs={{0,8},{8,16},{16,24},{24,32},{32,40},{40,48},{48,56},{56,64},{64,7... | collective-permute-start | bytes 589832 | tf_op jit(solution)/shard_map/while/body/eval_jaxpr/ppermute | solution.py:29
  294.9 11.6 %collective-permute-start = (f32[6,64,128]{2,1,0:T(8,128)S(1)}, f32[6,64,128]{2,1,0:T(8,128)S(1)}, u32[]{:S(2)}, u32[]{:S(2)}) collective-permute-start(f32[6,64,128]{2,1,0:T(8,128)S(1)} %bitcast_add_fusion.8), channel_id=1, source_target_pairs={{0,8},{8,16},{16,24},{24,32},{32,40},{40,48},{48,56},{56,64},{64,7... | collective-permute-start | bytes 589832 | tf_op jit(solution)/shard_map/while/body/eval_jaxpr/ppermute | solution.py:29
  308.0 10.9 %collective-permute-start = (f32[6,64,128]{2,1,0:T(8,128)S(1)}, f32[6,64,128]{2,1,0:T(8,128)S(1)}, u32[]{:S(2)}, u32[]{:S(2)}) collective-permute-start(f32[6,64,128]{2,1,0:T(8,128)S(1)} %bitcast_add_fusion.8), channel_id=1, source_target_pairs={{0,8},{8,16},{16,24},{24,32},{32,40},{40,48},{48,56},{56,64},{64,7... | collective-permute-start | bytes 589832 | tf_op jit(solution)/shard_map/while/body/eval_jaxpr/ppermute | solution.py:29
  320.3 10.1 %collective-permute-start = (f32[6,64,128]{2,1,0:T(8,128)S(1)}, f32[6,64,128]{2,1,0:T(8,128)S(1)}, u32[]{:S(2)}, u32[]{:S(2)}) collective-permute-start(f32[6,64,128]{2,1,0:T(8,128)S(1)} %bitcast_add_fusion.8), channel_id=1, source_target_pairs={{0,8},{8,16},{16,24},{24,32},{32,40},{40,48},{48,56},{56,64},{64,7... | collective-permute-start | bytes 589832 | tf_op jit(solution)/shard_map/while/body/eval_jaxpr/ppermute | solution.py:29
  331.8 9.7 %collective-permute-start = (f32[6,64,128]{2,1,0:T(8,128)S(1)}, f32[6,64,128]{2,1,0:T(8,128)S(1)}, u32[]{:S(2)}, u32[]{:S(2)}) collective-permute-start(f32[6,64,128]{2,1,0:T(8,128)S(1)} %bitcast_add_fusion.8), channel_id=1, source_target_pairs={{0,8},{8,16},{16,24},{24,32},{32,40},{40,48},{48,56},{56,64},{64,7... | collective-permute-start | bytes 589832 | tf_op jit(solution)/shard_map/while/body/eval_jaxpr/ppermute | solution.py:29
  343.0 9.7 %collective-permute-start = (f32[6,64,128]{2,1,0:T(8,128)S(1)}, f32[6,64,128]{2,1,0:T(8,128)S(1)}, u32[]{:S(2)}, u32[]{:S(2)}) collective-permute-start(f32[6,64,128]{2,1,0:T(8,128)S(1)} %bitcast_add_fusion.8), channel_id=1, source_target_pairs={{0,8},{8,16},{16,24},{24,32},{32,40},{40,48},{48,56},{56,64},{64,7... | collective-permute-start | bytes 589832 | tf_op jit(solution)/shard_map/while/body/eval_jaxpr/ppermute | solution.py:29
  354.1 9.7 %collective-permute-start = (f32[6,64,128]{2,1,0:T(8,128)S(1)}, f32[6,64,128]{2,1,0:T(8,128)S(1)}, u32[]{:S(2)}, u32[]{:S(2)}) collective-permute-start(f32[6,64,128]{2,1,0:T(8,128)S(1)} %bitcast_add_fusion.8), channel_id=1, source_target_pairs={{0,8},{8,16},{16,24},{24,32},{32,40},{40,48},{48,56},{56,64},{64,7... | collective-permute-start | bytes 589832 | tf_op jit(solution)/shard_map/while/body/eval_jaxpr/ppermute | solution.py:29
  365.2 9.7 %collective-permute-start = (f32[6,64,128]{2,1,0:T(8,128)S(1)}, f32[6,64,128]{2,1,0:T(8,128)S(1)}, u32[]{:S(2)}, u32[]{:S(2)}) collective-permute-start(f32[6,64,128]{2,1,0:T(8,128)S(1)} %bitcast_add_fusion.8), channel_id=1, source_target_pairs={{0,8},{8,16},{16,24},{24,32},{32,40},{40,48},{48,56},{56,64},{64,7... | collective-permute-start | bytes 589832 | tf_op jit(solution)/shard_map/while/body/eval_jaxpr/ppermute | solution.py:29
  376.3 9.7 %collective-permute-start = (f32[6,64,128]{2,1,0:T(8,128)S(1)}, f32[6,64,128]{2,1,0:T(8,128)S(1)}, u32[]{:S(2)}, u32[]{:S(2)}) collective-permute-start(f32[6,64,128]{2,1,0:T(8,128)S(1)} %bitcast_add_fusion.8), channel_id=1, source_target_pairs={{0,8},{8,16},{16,24},{24,32},{32,40},{40,48},{48,56},{56,64},{64,7... | collective-permute-start | bytes 589832 | tf_op jit(solution)/shard_map/while/body/eval_jaxpr/ppermute | solution.py:29
  387.4 10.1 %collective-permute-start = (f32[6,64,128]{2,1,0:T(8,128)S(1)}, f32[6,64,128]{2,1,0:T(8,128)S(1)}, u32[]{:S(2)}, u32[]{:S(2)}) collective-permute-start(f32[6,64,128]{2,1,0:T(8,128)S(1)} %bitcast_add_fusion.8), channel_id=1, source_target_pairs={{0,8},{8,16},{16,24},{24,32},{32,40},{40,48},{48,56},{56,64},{64,7... | collective-permute-start | bytes 589832 | tf_op jit(solution)/shard_map/while/body/eval_jaxpr/ppermute | solution.py:29
  399.0 11.3 %collective-permute-start = (f32[6,64,128]{2,1,0:T(8,128)S(1)}, f32[6,64,128]{2,1,0:T(8,128)S(1)}, u32[]{:S(2)}, u32[]{:S(2)}) collective-permute-start(f32[6,64,128]{2,1,0:T(8,128)S(1)} %bitcast_add_fusion.8), channel_id=1, source_target_pairs={{0,8},{8,16},{16,24},{24,32},{32,40},{40,48},{48,56},{56,64},{64,7... | collective-permute-start | bytes 589832 | tf_op jit(solution)/shard_map/while/body/eval_jaxpr/ppermute | solution.py:29
  411.7 11.1 %collective-permute-start = (f32[6,64,128]{2,1,0:T(8,128)S(1)}, f32[6,64,128]{2,1,0:T(8,128)S(1)}, u32[]{:S(2)}, u32[]{:S(2)}) collective-permute-start(f32[6,64,128]{2,1,0:T(8,128)S(1)} %bitcast_add_fusion.8), channel_id=1, source_target_pairs={{0,8},{8,16},{16,24},{24,32},{32,40},{40,48},{48,56},{56,64},{64,7... | collective-permute-start | bytes 589832 | tf_op jit(solution)/shard_map/while/body/eval_jaxpr/ppermute | solution.py:29
  424.3 10.3 %collective-permute-start = (f32[6,64,128]{2,1,0:T(8,128)S(1)}, f32[6,64,128]{2,1,0:T(8,128)S(1)}, u32[]{:S(2)}, u32[]{:S(2)}) collective-permute-start(f32[6,64,128]{2,1,0:T(8,128)S(1)} %bitcast_add_fusion.8), channel_id=1, source_target_pairs={{0,8},{8,16},{16,24},{24,32},{32,40},{40,48},{48,56},{56,64},{64,7... | collective-permute-start | bytes 589832 | tf_op jit(solution)/shard_map/while/body/eval_jaxpr/ppermute | solution.py:29
  436.0 9.7 %collective-permute-start = (f32[6,64,128]{2,1,0:T(8,128)S(1)}, f32[6,64,128]{2,1,0:T(8,128)S(1)}, u32[]{:S(2)}, u32[]{:S(2)}) collective-permute-start(f32[6,64,128]{2,1,0:T(8,128)S(1)} %bitcast_add_fusion.8), channel_id=1, source_target_pairs={{0,8},{8,16},{16,24},{24,32},{32,40},{40,48},{48,56},{56,64},{64,7... | collective-permute-start | bytes 589832 | tf_op jit(solution)/shard_map/while/body/eval_jaxpr/ppermute | solution.py:29
  446.1 3.6 copy-start.3
  465.1 6.0 copy-start.1
  473.9 10.9 %collective-permute-start.1 = (f32[6,64,128]{2,1,0:T(8,128)}, f32[6,64,128]{2,1,0:T(8,128)}, u32[]{:S(2)}, u32[]{:S(2)}) collective-permute-start(f32[6,64,128]{2,1,0:T(8,128)} %bitcast_add_fusion.9), channel_id=1, source_target_pairs={{8,0},{16,8},{24,16},{32,24},{40,32},{48,40},{56,48},{64,56},{72,6... | collective-permute-start | bytes 589832 | tf_op jit(solution)/shard_map/while/body/eval_jaxpr/ppermute | solution.py:29
  487.4 10.0 %collective-permute-start.1 = (f32[6,64,128]{2,1,0:T(8,128)}, f32[6,64,128]{2,1,0:T(8,128)}, u32[]{:S(2)}, u32[]{:S(2)}) collective-permute-start(f32[6,64,128]{2,1,0:T(8,128)} %bitcast_add_fusion.9), channel_id=1, source_target_pairs={{8,0},{16,8},{24,16},{32,24},{40,32},{48,40},{56,48},{64,56},{72,6... | collective-permute-start | bytes 589832 | tf_op jit(solution)/shard_map/while/body/eval_jaxpr/ppermute | solution.py:29
  500.1 10.0 %collective-permute-start.1 = (f32[6,64,128]{2,1,0:T(8,128)}, f32[6,64,128]{2,1,0:T(8,128)}, u32[]{:S(2)}, u32[]{:S(2)}) collective-permute-start(f32[6,64,128]{2,1,0:T(8,128)} %bitcast_add_fusion.9), channel_id=1, source_target_pairs={{8,0},{16,8},{24,16},{32,24},{40,32},{48,40},{56,48},{64,56},{72,6... | collective-permute-start | bytes 589832 | tf_op jit(solution)/shard_map/while/body/eval_jaxpr/ppermute | solution.py:29
  512.8 10.0 %collective-permute-start.1 = (f32[6,64,128]{2,1,0:T(8,128)}, f32[6,64,128]{2,1,0:T(8,128)}, u32[]{:S(2)}, u32[]{:S(2)}) collective-permute-start(f32[6,64,128]{2,1,0:T(8,128)} %bitcast_add_fusion.9), channel_id=1, source_target_pairs={{8,0},{16,8},{24,16},{32,24},{40,32},{48,40},{56,48},{64,56},{72,6... | collective-permute-start | bytes 589832 | tf_op jit(solution)/shard_map/while/body/eval_jaxpr/ppermute | solution.py:29
  525.5 10.0 %collective-permute-start.1 = (f32[6,64,128]{2,1,0:T(8,128)}, f32[6,64,128]{2,1,0:T(8,128)}, u32[]{:S(2)}, u32[]{:S(2)}) collective-permute-start(f32[6,64,128]{2,1,0:T(8,128)} %bitcast_add_fusion.9), channel_id=1, source_target_pairs={{8,0},{16,8},{24,16},{32,24},{40,32},{48,40},{56,48},{64,56},{72,6... | collective-permute-start | bytes 589832 | tf_op jit(solution)/shard_map/while/body/eval_jaxpr/ppermute | solution.py:29
  538.1 10.0 %collective-permute-start.1 = (f32[6,64,128]{2,1,0:T(8,128)}, f32[6,64,128]{2,1,0:T(8,128)}, u32[]{:S(2)}, u32[]{:S(2)}) collective-permute-start(f32[6,64,128]{2,1,0:T(8,128)} %bitcast_add_fusion.9), channel_id=1, source_target_pairs={{8,0},{16,8},{24,16},{32,24},{40,32},{48,40},{56,48},{64,56},{72,6... | collective-permute-start | bytes 589832 | tf_op jit(solution)/shard_map/while/body/eval_jaxpr/ppermute | solution.py:29
  550.8 10.0 %collective-permute-start.1 = (f32[6,64,128]{2,1,0:T(8,128)}, f32[6,64,128]{2,1,0:T(8,128)}, u32[]{:S(2)}, u32[]{:S(2)}) collective-permute-start(f32[6,64,128]{2,1,0:T(8,128)} %bitcast_add_fusion.9), channel_id=1, source_target_pairs={{8,0},{16,8},{24,16},{32,24},{40,32},{48,40},{56,48},{64,56},{72,6... | collective-permute-start | bytes 589832 | tf_op jit(solution)/shard_map/while/body/eval_jaxpr/ppermute | solution.py:29
  563.5 10.0 %collective-permute-start.1 = (f32[6,64,128]{2,1,0:T(8,128)}, f32[6,64,128]{2,1,0:T(8,128)}, u32[]{:S(2)}, u32[]{:S(2)}) collective-permute-start(f32[6,64,128]{2,1,0:T(8,128)} %bitcast_add_fusion.9), channel_id=1, source_target_pairs={{8,0},{16,8},{24,16},{32,24},{40,32},{48,40},{56,48},{64,56},{72,6... | collective-permute-start | bytes 589832 | tf_op jit(solution)/shard_map/while/body/eval_jaxpr/ppermute | solution.py:29
  576.2 11.1 %collective-permute-start.1 = (f32[6,64,128]{2,1,0:T(8,128)}, f32[6,64,128]{2,1,0:T(8,128)}, u32[]{:S(2)}, u32[]{:S(2)}) collective-permute-start(f32[6,64,128]{2,1,0:T(8,128)} %bitcast_add_fusion.9), channel_id=1, source_target_pairs={{8,0},{16,8},{24,16},{32,24},{40,32},{48,40},{56,48},{64,56},{72,6... | collective-permute-start | bytes 589832 | tf_op jit(solution)/shard_map/while/body/eval_jaxpr/ppermute | solution.py:29
  590.0 11.9 %collective-permute-start.1 = (f32[6,64,128]{2,1,0:T(8,128)}, f32[6,64,128]{2,1,0:T(8,128)}, u32[]{:S(2)}, u32[]{:S(2)}) collective-permute-start(f32[6,64,128]{2,1,0:T(8,128)} %bitcast_add_fusion.9), channel_id=1, source_target_pairs={{8,0},{16,8},{24,16},{32,24},{40,32},{48,40},{56,48},{64,56},{72,6... | collective-permute-start | bytes 589832 | tf_op jit(solution)/shard_map/while/body/eval_jaxpr/ppermute | solution.py:29
  604.6 11.0 %collective-permute-start.1 = (f32[6,64,128]{2,1,0:T(8,128)}, f32[6,64,128]{2,1,0:T(8,128)}, u32[]{:S(2)}, u32[]{:S(2)}) collective-permute-start(f32[6,64,128]{2,1,0:T(8,128)} %bitcast_add_fusion.9), channel_id=1, source_target_pairs={{8,0},{16,8},{24,16},{32,24},{40,32},{48,40},{56,48},{64,56},{72,6... | collective-permute-start | bytes 589832 | tf_op jit(solution)/shard_map/while/body/eval_jaxpr/ppermute | solution.py:29
  618.3 10.2 %collective-permute-start.1 = (f32[6,64,128]{2,1,0:T(8,128)}, f32[6,64,128]{2,1,0:T(8,128)}, u32[]{:S(2)}, u32[]{:S(2)}) collective-permute-start(f32[6,64,128]{2,1,0:T(8,128)} %bitcast_add_fusion.9), channel_id=1, source_target_pairs={{8,0},{16,8},{24,16},{32,24},{40,32},{48,40},{56,48},{64,56},{72,6... | collective-permute-start | bytes 589832 | tf_op jit(solution)/shard_map/while/body/eval_jaxpr/ppermute | solution.py:29
  631.2 10.0 %collective-permute-start.1 = (f32[6,64,128]{2,1,0:T(8,128)}, f32[6,64,128]{2,1,0:T(8,128)}, u32[]{:S(2)}, u32[]{:S(2)}) collective-permute-start(f32[6,64,128]{2,1,0:T(8,128)} %bitcast_add_fusion.9), channel_id=1, source_target_pairs={{8,0},{16,8},{24,16},{32,24},{40,32},{48,40},{56,48},{64,56},{72,6... | collective-permute-start | bytes 589832 | tf_op jit(solution)/shard_map/while/body/eval_jaxpr/ppermute | solution.py:29
  643.8 10.0 %collective-permute-start.1 = (f32[6,64,128]{2,1,0:T(8,128)}, f32[6,64,128]{2,1,0:T(8,128)}, u32[]{:S(2)}, u32[]{:S(2)}) collective-permute-start(f32[6,64,128]{2,1,0:T(8,128)} %bitcast_add_fusion.9), channel_id=1, source_target_pairs={{8,0},{16,8},{24,16},{32,24},{40,32},{48,40},{56,48},{64,56},{72,6... | collective-permute-start | bytes 589832 | tf_op jit(solution)/shard_map/while/body/eval_jaxpr/ppermute | solution.py:29
  656.5 10.0 %collective-permute-start.1 = (f32[6,64,128]{2,1,0:T(8,128)}, f32[6,64,128]{2,1,0:T(8,128)}, u32[]{:S(2)}, u32[]{:S(2)}) collective-permute-start(f32[6,64,128]{2,1,0:T(8,128)} %bitcast_add_fusion.9), channel_id=1, source_target_pairs={{8,0},{16,8},{24,16},{32,24},{40,32},{48,40},{56,48},{64,56},{72,6... | collective-permute-start | bytes 589832 | tf_op jit(solution)/shard_map/while/body/eval_jaxpr/ppermute | solution.py:29
  672.0 0.7 copy-start.5
